TPU v7x, 512 devices: a whole 4x8x8 slice. The times are simulated.
512 devices in a mesh: va: 32 (over x_lo, y, core), vb: 16 (over x_hi, z).
Axes of the slice: x: 4 (x_hi: 2, x_lo: 2; x = x_hi * 2 + x_lo), y: 8, z: 8, core: 2. Of those that a mesh axis runs over, the one named last changes fastest.
Arguments:
- amplitudes: bfloat16 [1024, 8, 65536], P('va', None, 'vb'), may hold values from -6 to 6
- integrals: bfloat16 [1024, 65536], P('va', 'vb'), may hold values from -0.125 to 0.125
- irrep_virt: int32 [1024], replicated, may hold values from 0 to 7
- irrep_occ: int32 [64], replicated, may hold values from 0 to 7, as said below
- irrep_slab: int32 [8], replicated, may hold values from 0 to 7
Outputs:
- cycle_term: bfloat16 [1024, 8192], P('vb', 'va')
Inputs may be any that keep to these rules, and one draw needn't show every extreme that they name: `irrep_virt`: D2h irrep labels. `irrep_occ`: D2h irrep labels; each aligned group of 8 consecutive orbitals k holds every label exactly once. `irrep_slab`: D2h irrep labels.
All inputs are finite; a program needn't handle non-finite values.
Results may differ from a plain program's by a relative error of at most 0.0015.
Values may be sent and summed in bfloat16 or wider, within the bound.
No kernel may reach another device: no remote copies, remote signals or barrier semaphores. Data moves between devices by JAX's collectives and lax.ppermute only.
A program may use at most 64 MiB of HBM per device.

v0:
```python
import jax
import jax.numpy as jnp
from jax import lax
from jax.sharding import PartitionSpec as P


def per_device(amplitudes, integrals, irrep_virt, irrep_occ, irrep_slab):
    a_rows, slab_count, pair_local = amplitudes.shape
    occ_count = irrep_occ.shape[0]
    c_local = pair_local // occ_count
    irr_first = lax.dynamic_slice_in_dim(irrep_virt, lax.axis_index("va") * a_rows, a_rows, 0)
    irr_second = lax.dynamic_slice_in_dim(irrep_virt, lax.axis_index("vb") * c_local, c_local, 0)
    pair_tag = jnp.bitwise_xor(irr_second[:, None], irrep_occ[None, :]).reshape(pair_local)
    left_tag = jnp.bitwise_xor(irr_first[:, None], irrep_slab[None, :])
    amp_sym = jnp.where(
        left_tag[:, :, None] == pair_tag[None, None, :], amplitudes, jnp.zeros_like(amplitudes)
    )
    flat_amp = amp_sym.reshape(a_rows * slab_count, pair_local)
    row_tag = jnp.bitwise_xor(irrep_virt, irrep_occ[0])
    gathered = lax.all_gather(integrals, "va", axis=0, tiled=True)
    int_sym = jnp.where(row_tag[:, None] == pair_tag[None, :], gathered, jnp.zeros_like(gathered))
    summed = lax.psum_scatter(
        lax.dot_general(
            int_sym, flat_amp, (((1,), (1,)), ((), ())), preferred_element_type=jnp.float32
        ),
        "vb",
        scatter_dimension=0,
        tiled=True,
    )
    return summed.astype(jnp.bfloat16)


def solution(mesh):
    placed = (P("va", None, "vb"), P("va", "vb"), P(), P(), P())
    return jax.shard_map(
        per_device, mesh=mesh, in_specs=placed, out_specs=P("vb", "va"), check_vma=False
    )
```

profile of v0, /device:TPU:8, one launch (start us, length us, event | category | flops | bytes accessed | tf_op | source)
XLA Modules:
  0.0 310.7 jit_solution(5064224351063463156)
XLA Ops:
  6.5 0.0 all-gather.2.cloned.1.call-start
  6.5 0.7 all-gather.2.cloned.1.call-update
  7.3 0.0 reduce-scatter.2.cloned.1.call-start
  7.3 0.8 dynamic_slice.7
  8.1 0.8 dynamic_slice.6
  8.8 0.7 broadcast_xor_fusion
  9.6 0.1 xor.52
  9.6 1.3 broadcast_xor_fusion.2
  11.0 0.7 broadcast_xor_fusion.1
  11.7 76.8 %all-gather.2.cloned.1.call-done = bf16[1024,4096]{1,0:T(8,128)(2,1)} async-done(((bf16[32,4096]{1,0:T(8,128)(2,1)}), bf16[1024,4096]{1,0:T(8,128)(2,1)}) %all-gather.2.cloned.1.call-update) | async-done | bytes 8388624 | tf_op jit(solution)/shard_map/all_gather | solution.py:20
  88.5 8.0 %fusion = f32[1024,256]{1,0:T(8,128)} fusion(bf16[1024,4096]{1,0:T(8,128)(2,1)} %all-gather.2.cloned.1.call-done, s32[4096]{0:T(1024)S(1)} %xor.52, s32[1024]{0:T(1024)S(1)} %broadcast_xor_fusion.2, bf16[32,8,4096]{2,1,0:T(8,128)(2,1)} %param.5, s32[32,8]{1,0:T(8,128)S(1)} %broadcast_xor_fusion.1), kind=kOutput, calls=%fused_computation.1 | convolution fusion | flops 2157969408 | bytes 11555840 | tf_op jit(solution)/shard_map/dot_general | solution.py:23
  96.5 0.0 reduce-scatter.2.cloned.1.call-update
  96.6 205.8 %reduce-scatter.2.cloned.1.call-done = f32[64,256]{1,0:T(8,128)} async-done(((f32[1024,256]{1,0:T(8,128)}), f32[64,256]{1,0:T(8,128)}) %reduce-scatter.2.cloned.1.call-update) | async-done | bytes 65552 | tf_op jit(solution)/shard_map/reduce_scatter | solution.py:22
  302.4 1.5 convert_element_type.3
Async XLA Ops:
  6.5 82.0 %all-gather.2.cloned.1.call-start = ((), (), s32[]{:S(2)}) async-start(), calls=%async_computation.1 | async-start | bytes 8650752 | tf_op jit(solution)/shard_map/all_gather | solution.py:20
  7.3 295.1 %reduce-scatter.2.cloned.1.call-start = ((), (), s32[]{:S(2)}) async-start(), calls=%async_computation.2 | async-start | bytes 1114112 | tf_op jit(solution)/shard_map/reduce_scatter | solution.py:22
Sparse Core Ops, SparseCore 0:
  9.5 78.9 all-gather.1
  96.7 205.6 reduce-scatter.1
where the time goes:
time: 311 us
  waiting for transfers between devices  283 us (91%)
  between operations  13.4 us (4%)
  matrix products  7.99 us (3%)
  other arithmetic  4.25 us (1%)
    reduce_scatter x1, waiting for transfers between devices, per_device(): lax.psum_scatter(lax.dot_general(int_sym, flat_amp, (((1,), (1,)), ((), (...  206 us
    all_gather x1, waiting for transfers between devices, per_device(): gathered = lax.all_gather(integrals, 'va', axis=0, tiled=True)  76.8 us
    dot_general x1, matrix products, per_device(): lax.dot_general(int_sym, flat_amp, (((1,), (1,)), ((), ())), preferred_el...  7.99 us
  transfers between devices with their start and end apart: 2, of which 2 were waited for; matrix products, arithmetic and copies ran while one was open for 1% of the time, Pallas kernels for 0%

commit v1 on v0

--- a/solution.py
+++ b/solution.py
@@ -2,6 +2,11 @@
 import jax.numpy as jnp
 from jax import lax
 from jax.sharding import PartitionSpec as P
+
+
+def swapped_in(x, name, dim):
+    sent = jnp.stack([x] * lax.axis_size(name))
+    return jnp.concatenate(lax.all_to_all(sent, name, 0, 0), axis=dim)
 
 
 def per_device(amplitudes, integrals, irrep_virt, irrep_occ, irrep_slab):
@@ -17,7 +22,7 @@
     )
     flat_amp = amp_sym.reshape(a_rows * slab_count, pair_local)
     row_tag = jnp.bitwise_xor(irrep_virt, irrep_occ[0])
-    gathered = lax.all_gather(integrals, "va", axis=0, tiled=True)
+    gathered = swapped_in(integrals, "va", 0)
     int_sym = jnp.where(row_tag[:, None] == pair_tag[None, :], gathered, jnp.zeros_like(gathered))
     summed = lax.psum_scatter(
         lax.dot_general(

time: 311 us -> 440 us (1.41)
  waiting for transfers between devices: 283 us -> 393 us
  starting transfers between devices: 0.04 us -> 10.5 us
  other arithmetic: 4.25 us -> 10.2 us
    all_to_all x0 -> x1, waiting for transfers between devices: none -> 183 us  [swapped_in(): return jnp.concatenate(lax.all_to_all(sent, name, 0, 0), axis=dim)]
    all_gather x1 -> x0, waiting for transfers between devices: 76.8 us -> none  [per_device(): gathered = lax.all_gather(integrals, 'va', axis=0, tiled=True)]
    all_to_all x0 -> x1, starting transfers between devices: none -> 10.5 us  [swapped_in(): return jnp.concatenate(lax.all_to_all(sent, name, 0, 0), axis=dim)]
    select_n x0 -> x1, other arithmetic: none -> 8.57 us  [per_device(): jnp.where(row_tag[:, None] == pair_tag[None, :], gathered, jnp.zeros_like...]
    another operation x0 -> x1, local copies, waits for them, and re-layouts: none -> 5.22 us  [swapped_in(): sent = jnp.stack([x] * lax.axis_size(name))]
    reduce_scatter x1, waiting for transfers between devices: 206 us -> 210 us  [per_device(): lax.psum_scatter(lax.dot_general(int_sym, flat_amp, (((1,), (1,)), ((), (...]
  transfers between devices with their start and end apart: 2 -> 2, of which waited for: 2 -> 2; matrix products, arithmetic and copies ran while one was open for 1% -> 0% of each run, Pallas kernels for 0% -> 0%
where the time goes in v1:
time: 440 us
  waiting for transfers between devices  393 us (89%)
  between operations  13.4 us (3%)
  starting transfers between devices  10.5 us (2%)
  other arithmetic  10.2 us (2%)
  matrix products  6.79 us (2%)
  local copies, waits for them, and re-layouts  5.53 us (1%)
    reduce_scatter x1, waiting for transfers between devices, per_device(): lax.psum_scatter(lax.dot_general(int_sym, flat_amp, (((1,), (1,)), ((), (...  210 us
    all_to_all x1, waiting for transfers between devices, swapped_in(): return jnp.concatenate(lax.all_to_all(sent, name, 0, 0), axis=dim)  183 us
    all_to_all x1, starting transfers between devices, swapped_in(): return jnp.concatenate(lax.all_to_all(sent, name, 0, 0), axis=dim)  10.5 us
  transfers between devices with their start and end apart: 2, of which 2 were waited for; matrix products, arithmetic and copies ran while one was open for 0% of the time, Pallas kernels for 0%

profile of v1, /device:TPU:8, one launch (start us, length us, event | category | flops | bytes accessed | tf_op | source)
XLA Modules:
  0.0 439.7 jit_solution(11531956929320558907)
XLA Ops:
  6.5 5.2 %stack.2 = bf16[32,32,4096]{2,1,0:T(8,128)(2,1)} broadcast(bf16[32,4096]{1,0:T(8,128)(2,1)} %param.6), dimensions={1,2} | broadcast | bytes 8650752 | tf_op jit(solution)/shard_map/stack | solution.py:8
  11.8 0.0 copy-start
  11.8 0.0 copy-start.1
  11.8 0.0 copy-start.2
  11.8 10.5 %all-to-all-start = ((bf16[32,32,4096]{2,1,0:T(8,128)(2,1)}), bf16[32,32,4096]{2,1,0:T(8,128)(2,1)}, u32[]{:S(2)}, u32[]{:S(2)}) async-start(bf16[32,32,4096]{2,1,0:T(8,128)(2,1)} %stack.2), calls=%async_computation | async-start | bytes 16777216 | tf_op jit(solution)/shard_map/all_to_all | solution.py:9
  22.3 0.0 reduce-scatter.2.cloned.1.call-start
  22.3 0.0 copy-done
  22.3 0.1 dynamic_slice.6
  22.4 0.0 copy-done.1
  22.4 0.1 broadcast_xor_fusion
  22.5 0.1 xor.52
  22.6 0.1 eq.29
  22.7 0.1 dynamic_slice.7
  22.8 0.0 copy-done.2
  22.8 0.1 broadcast_xor_fusion.1
  22.8 0.0 copy-start.3
  22.8 182.7 %all-to-all-done = bf16[32,32,4096]{2,1,0:T(8,128)(2,1)} async-done(((bf16[32,32,4096]{2,1,0:T(8,128)(2,1)}), bf16[32,32,4096]{2,1,0:T(8,128)(2,1)}, u32[]{:S(2)}, u32[]{:S(2)}) %all-to-all-start) | async-done | bytes 8388640 | tf_op jit(solution)/shard_map/all_to_all | solution.py:9
  205.6 8.6 %compare_select_fusion = bf16[32,32,4096]{2,1,0:T(8,128)(2,1)} fusion(bf16[32,32,4096]{2,1,0:T(8,128)(2,1)} %all-to-all-done, s32[4096]{0:T(1024)S(1)} %xor.52, s32[32,32]{1,0:T(8,128)S(1)} %eq.29), kind=kLoop, calls=%fused_computation | loop fusion | flops 8388608 | bytes 16797696 | tf_op jit(solution)/shard_map/jit(_where)/select_n | solution.py:26
  214.1 0.0 copy-done.3
  214.1 6.8 %fusion.1 = f32[1024,256]{1,0:T(8,128)} fusion(bf16[1024,4096]{1,0:T(8,128)(2,1)} %bitcast.7, bf16[32,8,4096]{2,1,0:T(8,128)(2,1)S(1)} %copy-done.3, s32[4096]{0:T(1024)S(1)} %xor.52, s32[32,8]{1,0:T(8,128)S(1)} %broadcast_xor_fusion.1), kind=kOutput, calls=%fused_computation.3 | convolution fusion | flops 2149580800 | bytes 11551744 | tf_op jit(solution)/shard_map/dot_general | solution.py:28
  220.9 0.0 reduce-scatter.2.cloned.1.call-update
  221.0 210.4 %reduce-scatter.2.cloned.1.call-done = f32[64,256]{1,0:T(8,128)} async-done(((f32[1024,256]{1,0:T(8,128)}), f32[64,256]{1,0:T(8,128)}) %reduce-scatter.2.cloned.1.call-update) | async-done | bytes 65552 | tf_op jit(solution)/shard_map/reduce_scatter | solution.py:27
  431.4 1.5 convert_element_type.3
  (1 shorter events, 0.0 us)
Async XLA Ops:
  11.8 10.6 %copy-start = (s32[1024]{0:T(1024)S(1)}, s32[1024]{0:T(1024)}, u32[]{:S(2)}) copy-start(s32[1024]{0:T(1024)} %param.7) | copy-start | bytes 12292
  11.8 10.7 %copy-start.1 = (s32[64]{0:T(128)S(1)}, s32[64]{0:T(128)}, u32[]{:S(2)}) copy-start(s32[64]{0:T(128)} %param.8) | copy-start | bytes 772
  11.8 11.0 %copy-start.2 = (s32[8]{0:T(128)S(1)}, s32[8]{0:T(128)}, u32[]{:S(2)}) copy-start(s32[8]{0:T(128)} %param.9) | copy-start | bytes 100
  11.8 193.8 %all-to-all-start = ((bf16[32,32,4096]{2,1,0:T(8,128)(2,1)}), bf16[32,32,4096]{2,1,0:T(8,128)(2,1)}, u32[]{:S(2)}, u32[]{:S(2)}) async-start(bf16[32,32,4096]{2,1,0:T(8,128)(2,1)} %stack.2), calls=%async_computation | async-start | bytes 16777216 | tf_op jit(solution)/shard_map/all_to_all | solution.py:9
  22.3 409.1 %reduce-scatter.2.cloned.1.call-start = ((), (), s32[]{:S(2)}) async-start(), calls=%async_computation.2 | async-start | bytes 1114112 | tf_op jit(solution)/shard_map/reduce_scatter | solution.py:27
  22.8 191.3 %copy-start.3 = (bf16[32,8,4096]{2,1,0:T(8,128)(2,1)S(1)}, bf16[32,8,4096]{2,1,0:T(8,128)(2,1)}, u32[]{:S(2)}) copy-start(bf16[32,8,4096]{2,1,0:T(8,128)(2,1)} %param.5) | copy-start | bytes 6291460
Sparse Core Ops, SparseCore 0:
  221.1 210.2 reduce-scatter.1
